TPU v7x, 128 devices: a whole 4x4x4 slice. The times are simulated.
128 devices in a mesh: row: 8 (over x_hi, z), col: 16 (over x_lo, y, core).
Axes of the slice: x: 4 (x_hi: 2, x_lo: 2; x = x_hi * 2 + x_lo), y: 4, z: 4, core: 2. Of those that a mesh axis runs over, the one named last changes fastest.
Arguments:
- left: float32 [2, 8192, 2560], P(None, 'row', 'col'), may hold values from -6 to 6
- right: float32 [2, 2560, 8192], P(None, 'row', 'col'), may hold values from -0.078125 to 0.078125
- prefix_owner: int32 [64], replicated, may hold values from 0 to 63, each once
- qubit_order: int32 [7], replicated, may hold values from 0 to 6, each once
Outputs:
- relaid: float32 [2, 8192, 8192], P(None, ('row', 'col'))
Inputs may be any that keep to these rules, and one draw needn't show every extreme that they name: `prefix_owner`: each prefix has exactly one owner, each owner one prefix. `qubit_order`: each open qubit appears once.
All inputs are finite; a program needn't handle non-finite values.
Results may differ from a plain program's by a relative error of at most 0.00007.
Values sent between devices are 32-bit elements; how exact they have to be, the bound alone decides.
A program may use at most 192 MiB of HBM per device.

v0:
```python
import jax
import jax.numpy as jnp
import numpy as np
from jax import lax
from jax.sharding import Mesh
from jax.sharding import PartitionSpec as P

LOW_BITS = 7
PREFIXES = 64
ROW = ("xh", "z")
CHIPS = ("xl", "y")
CORE = "core"
COL = ("xl", "y", "core")


def inverse_owner(prefix_owner, prefixes):
    labels = jnp.arange(prefixes, dtype=jnp.int32)
    match = (prefix_owner[None, :] == labels[:, None]).astype(jnp.int32)
    return jnp.sum(match * labels[None, :], axis=1)


def inner_order(qubit_order, low_bits):
    span = 2**low_bits
    offset = jnp.arange(span, dtype=jnp.int32)
    bits = jnp.bitwise_and(jnp.right_shift(offset[:, None], qubit_order[None, :]), 1)
    powers = jnp.left_shift(jnp.ones((low_bits,), jnp.int32), jnp.arange(low_bits, dtype=jnp.int32))
    return jnp.sum(bits * powers[None, :], axis=1)


def permute_left(left, prefix_owner, qubit_order, row_count, col_count):
    _, rows, kcols = left.shape
    span = 2**LOW_BITS
    local = rows // span
    sub = span // row_count
    x = left.reshape(2, local, row_count, sub, kcols)
    x = lax.all_to_all(x, ROW, split_axis=2, concat_axis=2, tiled=True)
    x = x.reshape(2, local * row_count, sub, kcols)
    inv = inverse_owner(prefix_owner, PREFIXES)
    pick = inv % local * row_count + inv // local
    y = jnp.take(x, pick, axis=1)
    y = y.reshape(2, row_count, local, sub, kcols)
    y = lax.all_to_all(y, ROW, split_axis=1, concat_axis=1, tiled=True)
    y = y.reshape(2, row_count * local * sub, kcols)
    s = inner_order(qubit_order, LOW_BITS)
    o_local = jnp.arange(local, dtype=jnp.int32)
    idx = s[None, :] // sub * (local * sub) + o_local[:, None] * sub + s[None, :] % sub
    idx = idx.reshape(-1)
    return jnp.take(y, jnp.take(idx, part_order(rows, col_count)), axis=1)


def part_sizes(q_total):
    return [q_total * 3 // 4, q_total - q_total * 3 // 4]


def part_order(rows, col_count):
    q_total = rows // col_count
    pos = []
    off = 0
    for qp in part_sizes(q_total):
        for c in range(col_count):
            pos.extend((c * q_total + off + i for i in range(qp)))
        off += qp
    return np.asarray(pos, np.int32)


def body(left, right, prefix_owner, qubit_order):
    row_count = lax.axis_size(ROW)
    col_count = lax.axis_size(COL)
    rows = left.shape[1]
    cols = right.shape[2]
    rpiece = jnp.swapaxes(right, 0, 1).reshape(right.shape[1], 2 * cols)
    rall = lax.all_gather(rpiece, ROW, axis=0, tiled=True)
    lp = permute_left(left, prefix_owner, qubit_order, row_count, col_count)
    lt = jnp.swapaxes(lp, 1, 2)
    lt = lax.optimization_barrier((lt, rall))[0]
    high = lax.Precision.HIGH
    dims = (((0,), (0,)), ((), ()))
    dot = lambda a, b: lax.dot_general(
        a, b, dims, preferred_element_type=jnp.float32, precision=high
    )
    outs = []
    prev = None
    start = 0
    for qp in part_sizes(rows // col_count):
        part = qp * col_count
        piece = lt[:, :, start : start + part]
        start += part
        piece = jnp.swapaxes(piece, 0, 1).reshape(piece.shape[1], 2 * part)
        if prev is not None:
            piece = lax.optimization_barrier((piece, prev))[0]
        lall = lax.all_gather(piece, COL, axis=0, tiled=True)
        prev = lall
        q = dot(lall, rall)
        re = q[:part, :cols] - q[part:, cols:]
        im = q[:part, cols:] + q[part:, :cols]
        tile = jnp.stack([re, im], axis=0)
        tile = tile.reshape(2, col_count, qp, cols)
        outs.append(lax.all_to_all(tile, COL, split_axis=1, concat_axis=3, tiled=True))
    out = jnp.concatenate(outs, axis=2)
    return out.reshape(2, rows // col_count, col_count * cols)


def solution(mesh):
    devices = np.asarray(mesh.devices)
    nr, nc = devices.shape
    fine = Mesh(devices.reshape(2, nr // 2, 2, nc // 4, 2), ("xh", "z", "xl", "y", "core"))
    in_specs = (P(None, ROW, COL), P(None, ROW, COL), P(), P())
    out_specs = P(None, ROW + COL, None)
    return jax.shard_map(body, mesh=fine, in_specs=in_specs, out_specs=out_specs, check_vma=False)
```

profile of v0, /device:TPU:1, one launch (start us, length us, event | category | flops | bytes accessed | tf_op | source)
XLA Modules:
  0.0 377.7 jit_solution(4709633685626059220)
XLA Ops:
  6.5 2.6 copy.59
  11.6 8.5 %all-to-all-start = ((f32[2,8,8,16,160]{4,3,1,0,2:T(8,128)}), f32[2,8,8,16,160]{4,3,1,0,2:T(8,128)S(1)}, u32[]{:S(2)}, u32[]{:S(2)}) async-start(f32[2,8,8,16,160]{4,3,1,0,2:T(8,128)} %copy.45), calls=%async_computation | async-start | bytes 4194304 | tf_op jit(solution)/shard_map/all_to_all | solution.py:36
  20.4 39.1 %all-to-all-done = f32[2,8,8,16,160]{4,3,1,0,2:T(8,128)S(1)} async-done(((f32[2,8,8,16,160]{4,3,1,0,2:T(8,128)}), f32[2,8,8,16,160]{4,3,1,0,2:T(8,128)S(1)}, u32[]{:S(2)}, u32[]{:S(2)}) %all-to-all-start) | async-done | bytes 1310752 | tf_op jit(solution)/shard_map/all_to_all | solution.py:36
  61.1 2.3 gather_fusion.1
  64.9 4.1 %all-to-all-start.1 = ((f32[2,8,8,16,160]{4,3,2,0,1:T(8,128)}), f32[2,8,8,16,160]{4,3,2,0,1:T(8,128)S(1)}, u32[]{:S(2)}, u32[]{:S(2)}) async-start(f32[2,8,8,16,160]{4,3,2,0,1:T(8,128)} %copy_select_fusion), calls=%async_computation.1 | async-start | bytes 4194304 | tf_op jit(solution)/shard_map/all_to_all | solution.py:42
  69.2 4.5 %gather_fusion = s32[1024]{0:T(1024)S(1)} fusion(s32[1024]{0:T(1024)S(1)} %add_bitcast_fusion, s32[1024]{0:T(1024)S(1)} %broadcast_clamp_fusion), kind=kCustom, calls=%fused_computation | custom fusion | bytes 12288 | tf_op jit(solution)/shard_map/jit(_take)/gather | solution.py:48
  73.7 33.3 %all-to-all-done.1 = f32[2,8,8,16,160]{4,3,2,0,1:T(8,128)S(1)} async-done(((f32[2,8,8,16,160]{4,3,2,0,1:T(8,128)}), f32[2,8,8,16,160]{4,3,2,0,1:T(8,128)S(1)}, u32[]{:S(2)}, u32[]{:S(2)}) %all-to-all-start.1) | async-done | bytes 1310752 | tf_op jit(solution)/shard_map/all_to_all | solution.py:42
  107.2 2.9 copy.49
  110.1 5.8 %gather_fusion.2 = f32[1024,2,160]{2,1,0:T(2,128)S(1)} fusion(f32[2,1024,160]{2,0,1:T(2,128)} %copy.49, s32[1024]{0:T(1024)S(1)} %fusion.6), kind=kCustom, calls=%fused_computation.2 | custom fusion | bytes 2625536 | tf_op jit(solution)/shard_map/jit(_take)/gather | solution.py:48
  115.9 4.5 %select_bitcast_fusion = f32[2,160,1024]{1,0,2:T(2,128)} fusion(f32[1024,2,160]{2,1,0:T(2,128)S(1)} %gather_fusion.2, pred[1024]{0:T(1024)(128)(4,1)S(1)} %compare_and_fusion.1), kind=kLoop, calls=%fused_computation.6 | loop fusion | flops 327680 | bytes 2622464 | tf_op jit(solution)/shard_map/jit(_take)/select_n | solution.py:48
  120.4 49.8 %all-gather.4.cloned.1.call-done = f32[2560,1024]{1,0:T(8,128)} async-done(((f32[320,1024]{1,0:T(8,128)}), f32[2560,1024]{1,0:T(8,128)}) %all-gather.4.cloned.1.call-update) | async-done | bytes 10485776 | tf_op jit(solution)/shard_map/all_gather | solution.py:72
  170.2 1.9 slice_bitcast_fusion
  172.1 1.8 copy.51
  177.6 82.2 %all-gather.6.cloned.1.call-done = f32[2560,1536]{1,0:T(8,128)} async-done(((f32[160,1536]{1,0:T(8,128)}), f32[2560,1536]{1,0:T(8,128)}) %all-gather.6.cloned.1.call-update) | async-done | bytes 15728656 | tf_op jit(solution)/shard_map/all_gather | solution.py:91
  259.8 31.6 %fusion.11 = f32[1536,1024]{1,0:T(8,128)S(1)} fusion(f32[2560,1536]{1,0:T(8,128)} %all-gather.6.cloned.1.call-done, f32[2560,1024]{1,0:T(8,128)} %all-gather.4.cloned.1.call-done), kind=kOutput, calls=%fused_computation.55 | convolution fusion | flops 24159191040 | bytes 32505856 | tf_op jit(solution)/shard_map/dot_general | solution.py:78
  292.1 2.2 pad_maximum_fusion
  294.3 5.0 %all-to-all-start.2 = ((f32[2,16,48,512]{3,2,0,1:T(8,128)}), f32[2,16,48,512]{3,2,0,1:T(8,128)S(1)}, u32[]{:S(2)}, u32[]{:S(2)}) async-start(f32[2,16,48,512]{3,2,0,1:T(8,128)} %pad_maximum_fusion), calls=%async_computation.2 | async-start | bytes 6291456 | tf_op jit(solution)/shard_map/all_to_all | solution.py:98
  299.3 2.5 all-gather.8.cloned.1.call-done
  301.9 12.1 %fusion.12 = f32[512,1024]{1,0:T(8,128)S(1)} fusion(f32[2560,512]{1,0:T(8,128)} %all-gather.8.cloned.1.call-done, f32[2560,1024]{1,0:T(8,128)} %all-gather.4.cloned.1.call-done), kind=kOutput, calls=%fused_computation.56 | convolution fusion | flops 8053063680 | bytes 17825792 | tf_op jit(solution)/shard_map/dot_general | solution.py:78
  315.2 24.4 %all-to-all-done.2 = f32[2,16,48,512]{3,2,0,1:T(8,128)S(1)} async-done(((f32[2,16,48,512]{3,2,0,1:T(8,128)}), f32[2,16,48,512]{3,2,0,1:T(8,128)S(1)}, u32[]{:S(2)}, u32[]{:S(2)}) %all-to-all-start.2) | async-done | bytes 3145760 | tf_op jit(solution)/shard_map/all_to_all | solution.py:98
  339.7 10.1 %all-to-all-start.3 = ((f32[2,16,16,512]{3,2,0,1:T(8,128)}), f32[2,16,16,512]{3,2,0,1:T(8,128)}, u32[]{:S(2)}, u32[]{:S(2)}) async-start(f32[2,16,16,512]{3,2,0,1:T(8,128)} %pad_maximum_fusion.1), calls=%async_computation.3 | async-start | bytes 2097152 | tf_op jit(solution)/shard_map/all_to_all | solution.py:98
  349.7 2.1 copy.60
  351.8 13.8 %all-to-all-done.3 = f32[2,16,16,512]{3,2,0,1:T(8,128)} async-done(((f32[2,16,16,512]{3,2,0,1:T(8,128)}), f32[2,16,16,512]{3,2,0,1:T(8,128)}, u32[]{:S(2)}, u32[]{:S(2)}) %all-to-all-start.3) | async-done | bytes 1048608 | tf_op jit(solution)/shard_map/all_to_all | solution.py:98
  367.0 4.2 %maximum_bitcast_fusion = f32[2,64,8192]{2,1,0:T(8,128)} fusion(f32[2,1,16,8192]{3,2,0,1:T(8,128)S(1)} %bitcast.75, f32[2,1,48,8192]{3,2,0,1:T(8,128)} %bitcast.67), kind=kLoop, calls=%fused_computation.3 | loop fusion | flops 1048576 | bytes 8388608 | tf_op jit(solution)/shard_map/reshape | solution.py:100
  (40 shorter events, 13.1 us)
Async XLA Ops:
  6.5 2.7 copy-start
  6.5 163.6 %all-gather.4.cloned.1.call-start = ((), (), s32[]{:S(2)}) async-start(), calls=%async_computation.4 | async-start | bytes 11796480 | tf_op jit(solution)/shard_map/all_gather | solution.py:72
  11.6 8.5 %copy-start.2 = (s32[64]{0:T(128)S(1)}, s32[64]{0:T(128)}, u32[]{:S(2)}) copy-start(s32[64]{0:T(128)} %param.7) | copy-start | bytes 772
  11.6 8.7 %copy-start.3 = (s32[7]{0:T(128)S(1)}, s32[7]{0:T(128)}, u32[]{:S(2)}) copy-start(s32[7]{0:T(128)} %param.8) | copy-start | bytes 88
  11.6 47.9 %all-to-all-start = ((f32[2,8,8,16,160]{4,3,1,0,2:T(8,128)}), f32[2,8,8,16,160]{4,3,1,0,2:T(8,128)S(1)}, u32[]{:S(2)}, u32[]{:S(2)}) async-start(f32[2,8,8,16,160]{4,3,1,0,2:T(8,128)} %copy.45), calls=%async_computation | async-start | bytes 4194304 | tf_op jit(solution)/shard_map/all_to_all | solution.py:36
  64.9 4.3 %copy-start.1 = (s32[1024]{0:T(1024)S(1)}, s32[1024]{0:T(1024)}, u32[]{:S(2)}) copy-start(s32[1024]{0:T(1024)} %constant.116) | copy-start | bytes 12292
  64.9 42.1 %all-to-all-start.1 = ((f32[2,8,8,16,160]{4,3,2,0,1:T(8,128)}), f32[2,8,8,16,160]{4,3,2,0,1:T(8,128)S(1)}, u32[]{:S(2)}, u32[]{:S(2)}) async-start(f32[2,8,8,16,160]{4,3,2,0,1:T(8,128)} %copy_select_fusion), calls=%async_computation.1 | async-start | bytes 4194304 | tf_op jit(solution)/shard_map/all_to_all | solution.py:42
  69.0 190.8 %all-gather.6.cloned.1.call-start = ((), (), s32[]{:S(2)}) async-start(), calls=%async_computation.5 | async-start | bytes 16711680 | tf_op jit(solution)/shard_map/all_gather | solution.py:91
  174.9 126.9 %all-gather.8.cloned.1.call-start = ((), (), s32[]{:S(2)}) async-start(), calls=%async_computation.6 | async-start | bytes 5570560 | tf_op jit(solution)/shard_map/all_gather | solution.py:91
  294.3 45.3 %all-to-all-start.2 = ((f32[2,16,48,512]{3,2,0,1:T(8,128)}), f32[2,16,48,512]{3,2,0,1:T(8,128)S(1)}, u32[]{:S(2)}, u32[]{:S(2)}) async-start(f32[2,16,48,512]{3,2,0,1:T(8,128)} %pad_maximum_fusion), calls=%async_computation.2 | async-start | bytes 6291456 | tf_op jit(solution)/shard_map/all_to_all | solution.py:98
  339.7 26.0 %all-to-all-start.3 = ((f32[2,16,16,512]{3,2,0,1:T(8,128)}), f32[2,16,16,512]{3,2,0,1:T(8,128)}, u32[]{:S(2)}, u32[]{:S(2)}) async-start(f32[2,16,16,512]{3,2,0,1:T(8,128)} %pad_maximum_fusion.1), calls=%async_computation.3 | async-start | bytes 2097152 | tf_op jit(solution)/shard_map/all_to_all | solution.py:98
Sparse Core Ops, SparseCore 0:
  9.7 160.4 all-gather.3
  175.1 84.6 all-gather.5
  261.5 40.3 all-gather.7
where the time goes:
time: 378 us
  waiting for transfers between devices  245 us (65%)
  matrix products  43.7 us (12%)
  local copies, waits for them, and re-layouts  32.8 us (9%)
  starting transfers between devices  27.9 us (7%)
  other arithmetic  14.7 us (4%)
  between operations  13.3 us (4%)
    all_gather x2, waiting for transfers between devices, body(): lall = lax.all_gather(piece, COL, axis=0, tiled=True)  84.7 us
    all_gather x1, waiting for transfers between devices, body(): rall = lax.all_gather(rpiece, ROW, axis=0, tiled=True)  49.8 us
    dot_general x2, matrix products, body(): lax.dot_general(a, b, dims, preferred_element_type=jnp.float32, precision...  43.7 us
    all_to_all x1, waiting for transfers between devices, permute_left(): x = lax.all_to_all(x, ROW, split_axis=2, concat_axis=2, tiled=True)  39.1 us
    all_to_all x2, waiting for transfers between devices, body(): lax.all_to_all(tile, COL, split_axis=1, concat_axis=3, tiled=True)  38.3 us
    all_to_all x1, waiting for transfers between devices, permute_left(): y = lax.all_to_all(y, ROW, split_axis=1, concat_axis=1, tiled=True)  33.3 us
    all_to_all x2, starting transfers between devices, body(): lax.all_to_all(tile, COL, split_axis=1, concat_axis=3, tiled=True)  15.1 us
    gather x2, local copies, waits for them, and re-layouts, permute_left(): return jnp.take(y, jnp.take(idx, part_order(rows, col_count)), axis=1)  10.3 us
  transfers between devices with their start and end apart: 7, of which 7 were waited for; matrix products, arithmetic and copies ran while one was open for 21% of the time, Pallas kernels for 0%

commit v1 on v0

--- a/solution.py
+++ b/solution.py
@@ -69,7 +69,9 @@
     rows = left.shape[1]
     cols = right.shape[2]
     rpiece = jnp.swapaxes(right, 0, 1).reshape(right.shape[1], 2 * cols)
-    rall = lax.all_gather(rpiece, ROW, axis=0, tiled=True)
+    rall = jnp.concatenate(
+        lax.all_to_all(jnp.stack([rpiece] * lax.axis_size(ROW)), ROW, 0, 0), axis=0
+    )
     lp = permute_left(left, prefix_owner, qubit_order, row_count, col_count)
     lt = jnp.swapaxes(lp, 1, 2)
     lt = lax.optimization_barrier((lt, rall))[0]

time: 378 us -> 419 us (1.11)
  waiting for transfers between devices: 245 us -> 274 us
  starting transfers between devices: 27.9 us -> 34.3 us
  local copies, waits for them, and re-layouts: 32.8 us -> 37.9 us
    all_to_all x0 -> x1, waiting for transfers between devices: none -> 98 us  [body(): lax.all_to_all(jnp.stack([rpiece] * lax.axis_size(ROW)), ROW, 0, 0)]
    all_gather x1 -> x0, waiting for transfers between devices: 49.8 us -> none  [body(): rall = lax.all_gather(rpiece, ROW, axis=0, tiled=True)]
    all_to_all x1, waiting for transfers between devices: 39.1 us -> 25.9 us  [permute_left(): x = lax.all_to_all(x, ROW, split_axis=2, concat_axis=2, tiled=True)]
    all_to_all x1, waiting for transfers between devices: 33.3 us -> 24.7 us  [permute_left(): y = lax.all_to_all(y, ROW, split_axis=1, concat_axis=1, tiled=True)]
    another operation x0 -> x2, local copies, waits for them, and re-layouts: none -> 6.74 us  [body(): jnp.stack([rpiece] * lax.axis_size(ROW))]
    all_to_all x0 -> x1, starting transfers between devices: none -> 5.32 us  [body(): lax.all_to_all(jnp.stack([rpiece] * lax.axis_size(ROW)), ROW, 0, 0)]
  transfers between devices with their start and end apart: 7 -> 7, of which waited for: 7 -> 7; matrix products, arithmetic and copies ran while one was open for 21% -> 17% of each run, Pallas kernels for 0% -> 0%
where the time goes in v1:
time: 419 us; the launch traced here: 418 us
  waiting for transfers between devices  274 us (65%)
  matrix products  43.7 us (10%)
  local copies, waits for them, and re-layouts  37.9 us (9%)
  starting transfers between devices  34.3 us (8%)
  other arithmetic  14.7 us (4%)
  between operations  13.6 us (3%)
    all_to_all x1, waiting for transfers between devices, body(): lax.all_to_all(jnp.stack([rpiece] * lax.axis_size(ROW)), ROW, 0, 0)  98 us
    all_gather x2, waiting for transfers between devices, body(): lall = lax.all_gather(piece, COL, axis=0, tiled=True)  87.2 us
    dot_general x2, matrix products, body(): lax.dot_general(a, b, dims, preferred_element_type=jnp.float32, precision...  43.7 us
    all_to_all x2, waiting for transfers between devices, body(): lax.all_to_all(tile, COL, split_axis=1, concat_axis=3, tiled=True)  38.1 us
    all_to_all x1, waiting for transfers between devices, permute_left(): x = lax.all_to_all(x, ROW, split_axis=2, concat_axis=2, tiled=True)  25.9 us
    all_to_all x1, waiting for transfers between devices, permute_left(): y = lax.all_to_all(y, ROW, split_axis=1, concat_axis=1, tiled=True)  24.7 us
    all_to_all x2, starting transfers between devices, body(): lax.all_to_all(tile, COL, split_axis=1, concat_axis=3, tiled=True)  15.1 us
    gather x2, local copies, waits for them, and re-layouts, permute_left(): return jnp.take(y, jnp.take(idx, part_order(rows, col_count)), axis=1)  10.3 us
  transfers between devices with their start and end apart: 7, of which 7 were waited for; matrix products, arithmetic and copies ran while one was open for 17% of the time, Pallas kernels for 0%

profile of v1, /device:TPU:1, one launch (start us, length us, event | category | flops | bytes accessed | tf_op | source)
XLA Modules:
  0.0 418.2 jit_solution(9482001177819649438)
XLA Ops:
  9.9 8.5 %all-to-all-start = ((f32[2,8,8,16,160]{4,3,1,0,2:T(8,128)}), f32[2,8,8,16,160]{4,3,1,0,2:T(8,128)S(1)}, u32[]{:S(2)}, u32[]{:S(2)}) async-start(f32[2,8,8,16,160]{4,3,1,0,2:T(8,128)} %copy.45), calls=%async_computation | async-start | bytes 4194304 | tf_op jit(solution)/shard_map/all_to_all | solution.py:36
  18.6 25.9 %all-to-all-done = f32[2,8,8,16,160]{4,3,1,0,2:T(8,128)S(1)} async-done(((f32[2,8,8,16,160]{4,3,1,0,2:T(8,128)}), f32[2,8,8,16,160]{4,3,1,0,2:T(8,128)S(1)}, u32[]{:S(2)}, u32[]{:S(2)}) %all-to-all-start) | async-done | bytes 1310752 | tf_op jit(solution)/shard_map/all_to_all | solution.py:36
  46.0 2.3 gather_fusion.1
  49.9 5.2 %all-to-all-start.1 = ((f32[2,8,8,16,160]{4,3,2,0,1:T(8,128)}), f32[2,8,8,16,160]{4,3,2,0,1:T(8,128)S(1)}, u32[]{:S(2)}, u32[]{:S(2)}) async-start(f32[2,8,8,16,160]{4,3,2,0,1:T(8,128)} %copy_select_fusion), calls=%async_computation.1 | async-start | bytes 4194304 | tf_op jit(solution)/shard_map/all_to_all | solution.py:42
  56.5 24.7 %all-to-all-done.1 = f32[2,8,8,16,160]{4,3,2,0,1:T(8,128)S(1)} async-done(((f32[2,8,8,16,160]{4,3,2,0,1:T(8,128)}), f32[2,8,8,16,160]{4,3,2,0,1:T(8,128)S(1)}, u32[]{:S(2)}, u32[]{:S(2)}) %all-to-all-start.1) | async-done | bytes 1310752 | tf_op jit(solution)/shard_map/all_to_all | solution.py:42
  81.2 5.3 %stack.21 = f32[8,320,1024]{2,1,0:T(8,128)} broadcast(f32[320,1024]{1,0:T(8,128)S(1)} %bitcast.75), dimensions={1,2} | broadcast | bytes 11796480 | tf_op jit(solution)/shard_map/stack | solution.py:73
  86.5 5.3 %all-to-all-start.2 = ((f32[8,320,1024]{2,1,0:T(8,128)}), f32[8,320,1024]{2,1,0:T(8,128)}, u32[]{:S(2)}, u32[]{:S(2)}) async-start(f32[8,320,1024]{2,1,0:T(8,128)} %stack.21), calls=%async_computation.2 | async-start | bytes 20971520 | tf_op jit(solution)/shard_map/all_to_all | solution.py:73
  92.1 4.5 %gather_fusion = s32[1024]{0:T(1024)S(1)} fusion(s32[1024]{0:T(1024)S(1)} %add_bitcast_fusion, s32[1024]{0:T(1024)S(1)} %broadcast_clamp_fusion), kind=kCustom, calls=%fused_computation | custom fusion | bytes 12288 | tf_op jit(solution)/shard_map/jit(_take)/gather | solution.py:48
  96.9 2.9 copy.49
  99.8 5.8 %gather_fusion.2 = f32[1024,2,160]{2,1,0:T(2,128)S(1)} fusion(f32[2,1024,160]{2,0,1:T(2,128)} %copy.49, s32[1024]{0:T(1024)S(1)} %fusion.6), kind=kCustom, calls=%fused_computation.2 | custom fusion | bytes 2625536 | tf_op jit(solution)/shard_map/jit(_take)/gather | solution.py:48
  105.6 4.5 %select_bitcast_fusion = f32[2,160,1024]{1,0,2:T(2,128)} fusion(f32[1024,2,160]{2,1,0:T(2,128)S(1)} %gather_fusion.2, pred[1024]{0:T(1024)(128)(4,1)S(1)} %compare_and_fusion.1), kind=kLoop, calls=%fused_computation.6 | loop fusion | flops 327680 | bytes 2622464 | tf_op jit(solution)/shard_map/jit(_take)/select_n | solution.py:48
  110.0 98.0 %all-to-all-done.2 = f32[8,320,1024]{2,1,0:T(8,128)} async-done(((f32[8,320,1024]{2,1,0:T(8,128)}), f32[8,320,1024]{2,1,0:T(8,128)}, u32[]{:S(2)}, u32[]{:S(2)}) %all-to-all-start.2) | async-done | bytes 10485792 | tf_op jit(solution)/shard_map/all_to_all | solution.py:73
  208.0 1.9 slice_bitcast_fusion
  215.4 84.5 %all-gather.3.cloned.1.call-done = f32[2560,1536]{1,0:T(8,128)} async-done(((f32[160,1536]{1,0:T(8,128)}), f32[2560,1536]{1,0:T(8,128)}) %all-gather.3.cloned.1.call-update) | async-done | bytes 15728656 | tf_op jit(solution)/shard_map/all_gather | solution.py:93
  299.9 31.6 %fusion.11 = f32[1536,1024]{1,0:T(8,128)S(1)} fusion(f32[2560,1536]{1,0:T(8,128)} %all-gather.3.cloned.1.call-done, f32[2560,1024]{1,0:T(8,128)} %bitcast.10), kind=kOutput, calls=%fused_computation.55 | convolution fusion | flops 24159191040 | bytes 32505856 | tf_op jit(solution)/shard_map/dot_general | solution.py:80
  332.3 2.2 pad_maximum_fusion
  334.5 5.0 %all-to-all-start.3 = ((f32[2,16,48,512]{3,2,0,1:T(8,128)}), f32[2,16,48,512]{3,2,0,1:T(8,128)S(1)}, u32[]{:S(2)}, u32[]{:S(2)}) async-start(f32[2,16,48,512]{3,2,0,1:T(8,128)} %pad_maximum_fusion), calls=%async_computation.3 | async-start | bytes 6291456 | tf_op jit(solution)/shard_map/all_to_all | solution.py:100
  339.5 2.7 all-gather.5.cloned.1.call-done
  342.2 12.1 %fusion.12 = f32[512,1024]{1,0:T(8,128)S(1)} fusion(f32[2560,512]{1,0:T(8,128)} %all-gather.5.cloned.1.call-done, f32[2560,1024]{1,0:T(8,128)} %bitcast.10), kind=kOutput, calls=%fused_computation.56 | convolution fusion | flops 8053063680 | bytes 17825792 | tf_op jit(solution)/shard_map/dot_general | solution.py:80
  355.6 24.2 %all-to-all-done.3 = f32[2,16,48,512]{3,2,0,1:T(8,128)S(1)} async-done(((f32[2,16,48,512]{3,2,0,1:T(8,128)}), f32[2,16,48,512]{3,2,0,1:T(8,128)S(1)}, u32[]{:S(2)}, u32[]{:S(2)}) %all-to-all-start.3) | async-done | bytes 3145760 | tf_op jit(solution)/shard_map/all_to_all | solution.py:100
  379.8 10.1 %all-to-all-start.4 = ((f32[2,16,16,512]{3,2,0,1:T(8,128)}), f32[2,16,16,512]{3,2,0,1:T(8,128)}, u32[]{:S(2)}, u32[]{:S(2)}) async-start(f32[2,16,16,512]{3,2,0,1:T(8,128)} %pad_maximum_fusion.1), calls=%async_computation.4 | async-start | bytes 2097152 | tf_op jit(solution)/shard_map/all_to_all | solution.py:100
  389.9 2.1 copy.60
  392.0 13.8 %all-to-all-done.4 = f32[2,16,16,512]{3,2,0,1:T(8,128)} async-done(((f32[2,16,16,512]{3,2,0,1:T(8,128)}), f32[2,16,16,512]{3,2,0,1:T(8,128)}, u32[]{:S(2)}, u32[]{:S(2)}) %all-to-all-start.4) | async-done | bytes 1048608 | tf_op jit(solution)/shard_map/all_to_all | solution.py:100
  407.1 4.2 %maximum_bitcast_fusion = f32[2,64,8192]{2,1,0:T(8,128)} fusion(f32[2,1,16,8192]{3,2,0,1:T(8,128)S(1)} %bitcast.76, f32[2,1,48,8192]{3,2,0,1:T(8,128)} %bitcast.68), kind=kLoop, calls=%fused_computation.3 | loop fusion | flops 1048576 | bytes 8388608 | tf_op jit(solution)/shard_map/reshape | solution.py:102
  (38 shorter events, 17.3 us)
Async XLA Ops:
  9.9 8.5 %copy-start.1 = (s32[64]{0:T(128)S(1)}, s32[64]{0:T(128)}, u32[]{:S(2)}) copy-start(s32[64]{0:T(128)} %param.7) | copy-start | bytes 772
  9.9 34.6 %all-to-all-start = ((f32[2,8,8,16,160]{4,3,1,0,2:T(8,128)}), f32[2,8,8,16,160]{4,3,1,0,2:T(8,128)S(1)}, u32[]{:S(2)}, u32[]{:S(2)}) async-start(f32[2,8,8,16,160]{4,3,1,0,2:T(8,128)} %copy.45), calls=%async_computation | async-start | bytes 4194304 | tf_op jit(solution)/shard_map/all_to_all | solution.py:36
  49.9 31.4 %all-to-all-start.1 = ((f32[2,8,8,16,160]{4,3,2,0,1:T(8,128)}), f32[2,8,8,16,160]{4,3,2,0,1:T(8,128)S(1)}, u32[]{:S(2)}, u32[]{:S(2)}) async-start(f32[2,8,8,16,160]{4,3,2,0,1:T(8,128)} %copy_select_fusion), calls=%async_computation.1 | async-start | bytes 4194304 | tf_op jit(solution)/shard_map/all_to_all | solution.py:42
  86.5 5.4 %copy-start.2 = (s32[7]{0:T(128)S(1)}, s32[7]{0:T(128)}, u32[]{:S(2)}) copy-start(s32[7]{0:T(128)} %param.8) | copy-start | bytes 88
  86.5 5.6 %copy-start = (s32[1024]{0:T(1024)S(1)}, s32[1024]{0:T(1024)}, u32[]{:S(2)}) copy-start(s32[1024]{0:T(1024)} %constant.116) | copy-start | bytes 12292
  86.5 121.4 %all-to-all-start.2 = ((f32[8,320,1024]{2,1,0:T(8,128)}), f32[8,320,1024]{2,1,0:T(8,128)}, u32[]{:S(2)}, u32[]{:S(2)}) async-start(f32[8,320,1024]{2,1,0:T(8,128)} %stack.21), calls=%async_computation.2 | async-start | bytes 20971520 | tf_op jit(solution)/shard_map/all_to_all | solution.py:73
  91.9 208.0 %all-gather.3.cloned.1.call-start = ((), (), s32[]{:S(2)}) async-start(), calls=%async_computation.5 | async-start | bytes 16711680 | tf_op jit(solution)/shard_map/all_gather | solution.py:93
  212.7 129.4 %all-gather.5.cloned.1.call-start = ((), (), s32[]{:S(2)}) async-start(), calls=%async_computation.6 | async-start | bytes 5570560 | tf_op jit(solution)/shard_map/all_gather | solution.py:93
  334.5 45.3 %all-to-all-start.3 = ((f32[2,16,48,512]{3,2,0,1:T(8,128)}), f32[2,16,48,512]{3,2,0,1:T(8,128)S(1)}, u32[]{:S(2)}, u32[]{:S(2)}) async-start(f32[2,16,48,512]{3,2,0,1:T(8,128)} %pad_maximum_fusion), calls=%async_computation.3 | async-start | bytes 6291456 | tf_op jit(solution)/shard_map/all_to_all | solution.py:100
  379.8 26.0 %all-to-all-start.4 = ((f32[2,16,16,512]{3,2,0,1:T(8,128)}), f32[2,16,16,512]{3,2,0,1:T(8,128)}, u32[]{:S(2)}, u32[]{:S(2)}) async-start(f32[2,16,16,512]{3,2,0,1:T(8,128)} %pad_maximum_fusion.1), calls=%async_computation.4 | async-start | bytes 2097152 | tf_op jit(solution)/shard_map/all_to_all | solution.py:100
Sparse Core Ops, SparseCore 0:
  212.9 86.9 all-gather.2
  301.6 40.4 all-gather.4
